TPU v7x, 32 devices: a whole 2x2x4 slice. The times are simulated.
32 devices in a mesh: grp: 2 (over x), tile: 8 (over z, y), wave: 2 (over core).
Axes of the slice: x: 2, y: 2, z: 4, core: 2. Of those that a mesh axis runs over, the one named last changes fastest.
Arguments:
- residual: float32 [16, 8, 2, 8, 128], P(('grp', 'tile'), 'wave'), parts along dimension 0, may hold values from -210 to 210
- kernel: bfloat16 [16, 8, 9, 2, 128, 128], P(('grp', 'tile'), 'wave'), parts along dimension 0, may hold values from -0.125 to 0.125
- offsets: float32 [16, 8, 2, 128], P(('grp', 'tile'), 'wave'), parts along dimension 0, may hold values from 0 to 1
- neighbor: int32 [16, 8, 9], P(('grp', 'tile'), 'wave'), parts along dimension 0, may hold values from 0 to 8, each once within a row
- frequency: int32 [16], P('grp'), parts along dimension 0, may hold values from 0 to 7, each once
- lattice_x: int32 [128], replicated, may hold values from 0 to 127, each once
- lattice_y: int32 [128], replicated, may hold values from 0 to 127, each once
- spectral_weight: float32 [8, 128, 128], replicated, may hold values from 0.1 to 3
Outputs:
- image_two: float32 [16, 8, 2, 8, 128], P(('grp', 'tile'), 'wave'), parts along dimension 0
- arnoldi: float32 [8, 8], P('grp'), parts along dimension 0
There are 2 independent parts, one for each index of `grp`. A program takes and returns all parts, laid end to end along the dimension named above; an argument that names none is the same for every part. Nothing has to cross between parts.
Inputs may be any that keep to these rules, and one draw needn't show every extreme that they name: `neighbor`: each row names each of the nine neighbour slots once. `frequency`: each index appears once. `lattice_x`: each index appears once. `lattice_y`: each index appears once.
All inputs are finite; a program needn't handle non-finite values.
Results may differ from a plain program's by a relative error of at most 0.013.
Values may be sent and summed in bfloat16 or wider, within the bound.
A program may use at most 64 MiB of HBM per device.

v0:
```python
import math
import jax
import jax.numpy as jnp
from jax import lax
from jax.sharding import PartitionSpec as P

two_pi = 2.0 * math.pi
eps_norm = 1e-06


def padded_2(array, sides, width):
    for axis, dim in sides:
        size, length = (lax.axis_size(axis), array.shape[dim])
        up = [(i, (i + 1) % size) for i in range(size)]
        down = [(j, i) for i, j in up]
        last = lax.slice_in_dim(array, length - width, length, axis=dim)
        initial = lax.slice_in_dim(array, 0, width, axis=dim)
        before = lax.ppermute(last, axis, up)
        after = lax.ppermute(initial, axis, down)
        array = jnp.concatenate([before, array, after], axis=dim)
    return array


def phase_table(position, harmonic):
    phase_angle = two_pi * (position[:, None] * harmonic[None, :])
    return (jnp.cos(phase_angle).astype(jnp.bfloat16), jnp.sin(phase_angle).astype(jnp.bfloat16))


def project_rows(cosine_cols, sine_cols, twisted):
    row_count = cosine_cols.shape[1]
    stacked = jnp.concatenate([cosine_cols, sine_cols], 1)
    gram_matrix = lax.dot_general(
        stacked, twisted, (((0,), (0,)), ((), ())), preferred_element_type=jnp.float32
    )
    gram_matrix = gram_matrix.reshape(2, row_count, 2, -1)
    coef_real = gram_matrix[0, :, 0] + gram_matrix[1, :, 1]
    coef_imag = gram_matrix[0, :, 1] - gram_matrix[1, :, 0]
    return jnp.stack([coef_real, coef_imag], 1)


def expand_rows(cosine_cols, sine_cols, scaled):
    row_count = scaled.shape[0]
    upper_rows = scaled.reshape(row_count, -1)
    lower_rows = jnp.stack([-scaled[:, 1], scaled[:, 0]], 1).reshape(row_count, -1)
    matrix = jnp.concatenate([upper_rows, lower_rows], 0)
    stacked = jnp.concatenate([cosine_cols, sine_cols], 1)
    return jnp.dot(stacked, matrix, preferred_element_type=jnp.float32)


def twist_density(panel_density, cosine_y, sine_y):
    density_real = panel_density[:, 0, :, None].astype(jnp.float32)
    density_imag = panel_density[:, 1, :, None].astype(jnp.float32)
    wave_cos = cosine_y.astype(jnp.float32)[:, None, :]
    wave_sin = sine_y.astype(jnp.float32)[:, None, :]
    part_real = wave_cos * density_real + wave_sin * density_imag
    part_imag = wave_cos * density_imag - wave_sin * density_real
    return (
        jnp.stack([part_real, part_imag], 1)
        .reshape(panel_density.shape[0], -1)
        .astype(jnp.bfloat16)
    )


def finish(summed, cosine_y, sine_y, vectors):
    shaped = summed.reshape(summed.shape[0], 2, vectors, -1)
    wave_cos = cosine_y.astype(jnp.float32)[:, None, :]
    wave_sin = sine_y.astype(jnp.float32)[:, None, :]
    far_real = jnp.sum(shaped[:, 0] * wave_cos - shaped[:, 1] * wave_sin, -1)
    far_imag = jnp.sum(shaped[:, 0] * wave_sin + shaped[:, 1] * wave_cos, -1)
    return jnp.stack([far_real, far_imag], 1)


def combine_near(product, vectors):
    first_half = product[:, 0]
    second = product[:, 1]
    near_real = first_half[:, :vectors] - second[:, vectors:]
    near_imag = second[:, :vectors] + first_half[:, vectors:]
    return jnp.stack([near_real, near_imag], 1)


def panel_sum(values):
    return jnp.sum(values, axis=(0, 1, 3))


def per_device(
    residual, kernel, offsets, neighbor, frequency, lattice_x, lattice_y, spectral_weight
):
    strips = residual.shape[0]
    tiles_y = residual.shape[1]
    vectors = residual.shape[3]
    panels_t = residual.shape[4]
    modes_x = spectral_weight.shape[1]
    modes_y = spectral_weight.shape[2]
    count_x = lax.axis_size("tile") * strips
    count_y = lax.axis_size("wave") * tiles_y
    devices = lax.axis_size("tile") * lax.axis_size("wave")
    panels = count_x * count_y * panels_t
    local_rows = strips * tiles_y * panels_t
    column = (lax.axis_index("tile") * strips + jnp.arange(strips)).astype(jnp.float32)
    row_index = (lax.axis_index("wave") * tiles_y + jnp.arange(tiles_y)).astype(jnp.float32)
    position_x = ((column[:, None, None] + offsets[:, :, 0, :]) / count_x).reshape(-1)
    position_y = ((row_index[None, :, None] + offsets[:, :, 1, :]) / count_y).reshape(-1)
    harmonic_x = (lattice_x - modes_x // 2).astype(jnp.float32)
    harmonic_y = (lattice_y - modes_y // 2).astype(jnp.float32)
    cosine_x, sine_x = phase_table(position_x, harmonic_x)
    cosine_y, sine_y = phase_table(position_y, harmonic_y)
    weight_rows = jnp.take(spectral_weight, frequency, axis=0)
    factor = weight_rows * (1.0 / math.sqrt(modes_x * modes_y * panels))
    factor_wide = jnp.transpose(factor, (1, 0, 2)).reshape(modes_x, vectors * modes_y)[:, None, :]

    def near_field(density):
        padded = padded_2(density, (("tile", 0), ("wave", 1)), 1)
        candidates = []
        for slot_index in range(9):
            shift_x = slot_index // 3 - 1
            shift_y = slot_index % 3 - 1
            candidates.append(
                padded[1 + shift_x : 1 + shift_x + strips, 1 + shift_y : 1 + shift_y + tiles_y]
            )
        stacked = jnp.stack(candidates, 2).reshape(strips * tiles_y, 9, -1)
        picked = jnp.take_along_axis(stacked, neighbor.reshape(strips * tiles_y, 9, 1), axis=1)
        picked = picked.reshape(strips * tiles_y, 9, 2 * vectors, panels_t)
        blocks = kernel.reshape(strips * tiles_y, 9, 2, panels_t, panels_t)
        product = jnp.einsum("tjmp,tjcpq->tcmq", picked, blocks, preferred_element_type=jnp.float32)
        return combine_near(product, vectors).reshape(strips, tiles_y, 2, vectors, panels_t)

    def far_field(density):
        panel_density = jnp.transpose(density, (0, 1, 4, 2, 3)).reshape(local_rows, 2, vectors)
        twisted = twist_density(panel_density, cosine_y, sine_y)
        partial_coeffs = project_rows(cosine_x, sine_x, twisted)
        share_rows = modes_x // devices
        shares = lax.psum_scatter(partial_coeffs, ("tile", "wave"), scatter_dimension=0, tiled=True)
        owner_index = lax.axis_index("tile") * lax.axis_size("wave") + lax.axis_index("wave")
        owner_factor = lax.dynamic_slice_in_dim(
            factor_wide, owner_index * share_rows, share_rows, 0
        )
        owner_scaled = (shares * owner_factor).astype(jnp.bfloat16)
        scaled = lax.all_gather(owner_scaled, ("tile", "wave"), axis=0, tiled=True)
        summed = expand_rows(cosine_x, sine_x, scaled)
        far_panel = finish(summed, cosine_y, sine_y, vectors)
        return far_panel.reshape(strips, tiles_y, panels_t, 2, vectors).transpose(0, 1, 3, 4, 2)

    def apply_operator(density):
        return 0.5 * density.astype(jnp.float32) + near_field(density) + far_field(density)

    local_sq = panel_sum(
        residual[:, :, 0] * residual[:, :, 0] + residual[:, :, 1] * residual[:, :, 1]
    )
    squares = lax.psum(local_sq, ("tile", "wave"))
    basis_scale = jnp.sqrt(squares / panels + eps_norm)
    basis_one = (residual / basis_scale[None, None, None, :, None]).astype(jnp.bfloat16)
    image_one = apply_operator(basis_one)
    basis_real = basis_one[:, :, 0].astype(jnp.float32)
    basis_imag = basis_one[:, :, 1].astype(jnp.float32)
    image_real = image_one[:, :, 0]
    image_imag = image_one[:, :, 1]
    inner_real, inner_imag = lax.psum(
        (
            panel_sum(basis_real * image_real + basis_imag * image_imag),
            panel_sum(basis_real * image_imag - basis_imag * image_real),
        ),
        ("tile", "wave"),
    )
    coef_real = inner_real / panels
    coef_imag = inner_imag / panels
    wide_real = coef_real[None, None, :, None]
    wide_imag = coef_imag[None, None, :, None]
    update_real = image_real - (wide_real * basis_real - wide_imag * basis_imag)
    update_imag = image_imag - (wide_real * basis_imag + wide_imag * basis_real)
    update_sq = lax.psum(
        panel_sum(update_real * update_real + update_imag * update_imag), ("tile", "wave")
    )
    update_scale = jnp.sqrt(update_sq / panels + eps_norm)
    next_basis = (
        jnp.stack([update_real, update_imag], 2) / update_scale[None, None, None, :, None]
    ).astype(jnp.bfloat16)
    image_two = apply_operator(next_basis)
    arnoldi = jnp.stack([basis_scale, coef_real, coef_imag, update_scale])
    return (image_two, arnoldi)


def solution(mesh):
    return jax.shard_map(
        per_device,
        mesh=mesh,
        in_specs=(
            P(("grp", "tile"), "wave", None, None, None),
            P(("grp", "tile"), "wave", None, None, None, None),
            P(("grp", "tile"), "wave", None, None),
            P(("grp", "tile"), "wave", None),
            P("grp"),
            P(),
            P(),
            P(),
        ),
        out_specs=(P(("grp", "tile"), "wave", None, None, None), P("grp", None)),
        check_vma=False,
    )
```

profile of v0, /device:TPU:0, one launch (start us, length us, event | category | flops | bytes accessed | tf_op | source)
XLA Modules:
  0.0 307.0 jit_solution(9363511399105179548)
XLA Ops:
  7.2 1.0 add_reduce_fusion.2
  8.2 34.9 %psum.28 = f32[8]{0:T(128)S(1)} all-reduce(f32[8]{0:T(128)S(1)} %add_reduce_fusion.2), channel_id=1, replica_groups=mesh['grp'=2,'tile'=8,'wave'=2] {'tile','wave'}, use_global_device_ids=true, to_apply=%region_1.2 | all-reduce | flops 8 | bytes 64 | tf_op jit(solution)/shard_map/psum | solution.py:149
  43.7 1.4 fusion.22
  45.2 4.7 %collective-permute-start.1 = (bf16[1,4,2,8,128]{4,3,1,2,0:T(8,128)(2,1)}, bf16[1,4,2,8,128]{4,3,1,2,0:T(8,128)(2,1)}, u32[]{:S(2)}, u32[]{:S(2)}) collective-permute-start(bf16[1,4,2,8,128]{4,3,1,2,0:T(8,128)(2,1)} %fusion.22), channel_id=1, source_target_pairs={{2,0},{4,2},{6,4},{8,6},{10,8},{12,10},{14,12},{0,14},{3,1},{5,3},... | collective-permute-start | bytes 49160 | tf_op jit(solution)/shard_map/ppermute | solution.py:19
  49.9 0.8 fusion.72
  50.7 0.7 add_convert_fusion.2
  51.4 0.7 add_convert_fusion.4
  52.1 0.8 fusion.63
  52.9 1.0 fusion.16
  54.7 1.1 cosine_convert_fusion.1
  55.9 0.8 fusion.64
  56.9 1.1 pad_maximum_fusion.2
  58.1 0.6 shift-left_or_fusion
  58.7 1.6 gather_fusion
  60.3 0.9 multiply_bitcast_fusion
  61.7 1.2 copy.121
  63.0 1.3 pad_maximum_fusion.31
  64.3 1.0 constant_dynamic-slice_fusion
  65.3 0.8 copy.126
  66.2 0.9 copy.128
  67.0 0.7 copy.112
  67.8 1.2 copy.122
  69.0 0.8 reshape.723
  69.8 0.7 copy.109
  71.1 0.7 copy.115
  71.8 0.8 pad_maximum_fusion.21
  72.6 0.8 pad_maximum_fusion.18
  73.7 1.5 gather_fusion.1
  75.9 0.6 fusion.51
  76.5 36.3 %reduce-scatter.3.cloned.1.call-done = f32[8,2,1024]{2,0,1:T(8,128)} async-done(((f32[128,2,1024]{2,0,1:T(8,128)}), f32[8,2,1024]{2,0,1:T(8,128)}) %reduce-scatter.3.cloned.1.call-update) | async-done | bytes 65552 | tf_op jit(solution)/shard_map/reduce_scatter | solution.py:132
  112.8 0.8 multiply_convert_fusion.1
  113.7 20.8 %all_gather.6 = bf16[128,2,1024]{2,0,1:T(8,128)(2,1)S(1)} all-gather(bf16[8,2,1024]{2,0,1:T(8,128)(2,1)S(1)} %multiply_convert_fusion.1), channel_id=1, replica_groups=mesh['grp'=2,'tile'=8,'wave'=2] {'tile','wave'}, dimensions={0}, use_global_device_ids=true | all-gather | bytes 557056 | tf_op jit(solution)/shard_map/all_gather | solution.py:138
  134.4 0.8 slice_negate_fusion.1
  135.3 1.0 copy.123
  136.3 1.1 pad_maximum_fusion.4
  137.4 1.0 copy.124
  138.4 2.0 convolution_bitcast_fusion.1
  140.4 0.9 copy.178
  141.4 1.2 subtract_reduce_fusion.1
  142.6 0.7 copy.131
  143.4 0.9 fusion.19
  144.3 0.9 fusion.33
  145.2 29.8 %all-reduce = (f32[8]{0:T(128)S(1)}, f32[8]{0:T(128)S(1)}) all-reduce(f32[8]{0:T(128)S(1)} %get-tuple-element.16, f32[8]{0:T(128)S(1)} %get-tuple-element.15), channel_id=1, replica_groups=mesh['grp'=2,'tile'=8,'wave'=2] {'tile','wave'}, use_global_device_ids=true, to_apply=%region_8.10 | all-reduce | flops 16 | bytes 128 | tf_op jit(solution)/shard_map/psum | solution.py:157
  175.0 0.9 fusion.40
  175.9 0.8 fusion.45
  176.7 29.5 %psum.31 = f32[8]{0:T(128)S(1)} all-reduce(f32[8]{0:T(128)S(1)} %fusion.40), channel_id=1, replica_groups=mesh['grp'=2,'tile'=8,'wave'=2] {'tile','wave'}, use_global_device_ids=true, to_apply=%region_10.12 | all-reduce | flops 8 | bytes 64 | tf_op jit(solution)/shard_map/psum | solution.py:170
  206.4 4.7 %collective-permute-start.5 = (bf16[1,4,2,8,128]{4,3,1,2,0:T(8,128)(2,1)S(1)}, bf16[1,4,2,8,128]{4,3,1,2,0:T(8,128)(2,1)S(1)}, u32[]{:S(2)}, u32[]{:S(2)}) collective-permute-start(bf16[1,4,2,8,128]{4,3,1,2,0:T(8,128)(2,1)S(1)} %fusion.20), channel_id=1, source_target_pairs={{2,0},{4,2},{6,4},{8,6},{10,8},{12,10},{14,12},{0,14},{3,1},{5,3},... | collective-permute-start | bytes 49160 | tf_op jit(solution)/shard_map/ppermute | solution.py:19
  212.0 0.7 copy-done.8
  212.7 0.7 fusion.65
  213.7 1.1 pad_maximum_fusion.3
  214.9 0.6 pad_maximum_fusion.34
  216.1 0.7 collective-permute-done.6
  217.2 1.5 gather_fusion.2
  219.4 50.2 %reduce-scatter.5.cloned.1.call-done = f32[8,2,1024]{2,0,1:T(8,128)} async-done(((f32[128,2,1024]{2,0,1:T(8,128)}), f32[8,2,1024]{2,0,1:T(8,128)}) %reduce-scatter.5.cloned.1.call-update) | async-done | bytes 65552 | tf_op jit(solution)/shard_map/reduce_scatter | solution.py:132
  269.6 0.8 multiply_convert_fusion
  270.5 20.8 %all_gather.7 = bf16[128,2,1024]{2,0,1:T(8,128)(2,1)S(1)} all-gather(bf16[8,2,1024]{2,0,1:T(8,128)(2,1)S(1)} %multiply_convert_fusion), channel_id=1, replica_groups=mesh['grp'=2,'tile'=8,'wave'=2] {'tile','wave'}, dimensions={0}, use_global_device_ids=true | all-gather | bytes 557056 | tf_op jit(solution)/shard_map/all_gather | solution.py:138
  291.3 0.7 slice_negate_fusion
  292.0 1.0 copy.147
  293.0 1.0 pad_maximum_fusion.5
  294.0 1.0 copy.148
  295.1 2.0 convolution_bitcast_fusion
  297.0 0.9 copy.179
  298.1 1.2 subtract_reduce_fusion
  299.6 0.6 copy.155
  (157 shorter events, 7.2 us)
Async XLA Ops:
  7.2 68.3 %copy-start = (bf16[1,4,9,2,128,128]{5,4,3,2,1,0:T(8,128)(2,1)S(1)}, bf16[1,4,9,2,128,128]{5,4,3,2,1,0:T(8,128)(2,1)}, u32[]{:S(2)}) copy-start(bf16[1,4,9,2,128,128]{5,4,3,2,1,0:T(8,128)(2,1)} %param.11) | copy-start | bytes 7077892
  7.2 105.6 %reduce-scatter.3.cloned.1.call-start = ((), (), s32[]{:S(2)}) async-start(), calls=%async_computation.2 | async-start | bytes 1114112 | tf_op jit(solution)/shard_map/reduce_scatter | solution.py:132
  43.7 7.0 %copy-start.19 = (f32[8]{0:T(128)}, f32[8]{0:T(128)S(1)}, u32[]{:S(2)}) copy-start(f32[8]{0:T(128)S(1)} %get-tuple-element.68) | copy-start | bytes 100
  45.2 17.8 %collective-permute-start = (bf16[1,4,2,8,128]{4,3,1,2,0:T(8,128)(2,1)}, bf16[1,4,2,8,128]{4,3,1,2,0:T(8,128)(2,1)}, u32[]{:S(2)}, u32[]{:S(2)}) collective-permute-start(bf16[1,4,2,8,128]{4,3,1,2,0:T(8,128)(2,1)} %fusion.22), channel_id=1, source_target_pairs={{0,2},{2,4},{4,6},{6,8},{8,10},{10,12},{12,14},{14,0},{1,3},{3,5},... | collective-permute-start | bytes 49160 | tf_op jit(solution)/shard_map/ppermute | solution.py:18
  45.2 17.8 %collective-permute-start.1 = (bf16[1,4,2,8,128]{4,3,1,2,0:T(8,128)(2,1)}, bf16[1,4,2,8,128]{4,3,1,2,0:T(8,128)(2,1)}, u32[]{:S(2)}, u32[]{:S(2)}) collective-permute-start(bf16[1,4,2,8,128]{4,3,1,2,0:T(8,128)(2,1)} %fusion.22), channel_id=1, source_target_pairs={{2,0},{4,2},{6,4},{8,6},{10,8},{12,10},{14,12},{0,14},{3,1},{5,3},... | collective-permute-start | bytes 49160 | tf_op jit(solution)/shard_map/ppermute | solution.py:19
  53.9 12.3 %copy-start.1 = (f32[512,128]{0,1:T(8,128)}, f32[512,128]{0,1:T(8,128)S(1)}, u32[]{:S(2)}) copy-start(f32[512,128]{0,1:T(8,128)S(1)} %get-tuple-element.64) | copy-start | bytes 786436
  55.8 0.8 copy-start.9
  55.9 0.8 copy-start.7
  56.9 1.2 copy-start.24
  56.9 1.2 copy-start.18
  58.0 211.7 %reduce-scatter.5.cloned.1.call-start = ((), (), s32[]{:S(2)}) async-start(), calls=%async_computation.3 | async-start | bytes 1114112 | tf_op jit(solution)/shard_map/reduce_scatter | solution.py:132
  64.3 7.5 %collective-permute-start.2 = (bf16[3,1,2,8,128]{4,3,1,2,0:T(8,128)(2,1)}, bf16[3,1,2,8,128]{4,3,1,2,0:T(8,128)(2,1)}, u32[]{:S(2)}, u32[]{:S(2)}) collective-permute-start(bf16[3,1,2,8,128]{4,3,1,2,0:T(8,128)(2,1)} %get-tuple-element.56), channel_id=1, source_target_pairs={{0,1},{1,0},{2,3},{3,2},{4,5},{5,4},{6,7},{7,6},{8,9},{9,8},{10,11... | collective-permute-start | bytes 36872 | tf_op jit(solution)/shard_map/ppermute | solution.py:18
  67.7 7.5 %copy-start.21 = (pred[4,9]{1,0:T(4,128)(4,1)S(1)}, pred[4,9]{1,0:T(4,128)(4,1)}, u32[]{:S(2)}) copy-start(pred[4,9]{1,0:T(4,128)(4,1)} %and_bitcast_fusion) | copy-start | bytes 112
  69.0 43.9 %copy-start.16 = (f32[8,1,1024]{2,0,1:T(8,128)}, f32[8,1,1024]{2,0,1:T(8,128)S(1)}, u32[]{:S(2)}) copy-start(f32[8,1,1024]{2,0,1:T(8,128)S(1)} %copy.122) | copy-start | bytes 98308
  70.5 2.1 collective-permute-start.3
  134.4 4.0 %copy-start.10 = (bf16[512,128]{0,1:T(8,128)(2,1)S(1)}, bf16[512,128]{0,1:T(8,128)(2,1)}, u32[]{:S(2)}) copy-start(bf16[512,128]{0,1:T(8,128)(2,1)} %copy-done.9) | copy-start | bytes 393220
  140.4 1.0 copy-start.3
  140.4 1.0 copy-start.5
  141.4 2.0 copy-start.20
  141.4 69.8 %copy-start.2 = (f32[512,128]{0,1:T(8,128)S(1)}, f32[512,128]{0,1:T(8,128)}, u32[]{:S(2)}) copy-start(f32[512,128]{0,1:T(8,128)} %copy-done.1) | copy-start | bytes 786436
  176.7 38.0 %copy-start.12 = (f32[1,4,1,8,128]{4,3,1,2,0:T(8,128)}, f32[1,4,1,8,128]{4,3,1,2,0:T(8,128)S(1)}, u32[]{:S(2)}) copy-start(f32[1,4,1,8,128]{4,3,1,2,0:T(8,128)S(1)} %get-tuple-element.51) | copy-start | bytes 49156
  176.7 38.0 %copy-start.14 = (f32[1,4,1,8,128]{4,3,1,2,0:T(8,128)}, f32[1,4,1,8,128]{4,3,1,2,0:T(8,128)S(1)}, u32[]{:S(2)}) copy-start(f32[1,4,1,8,128]{4,3,1,2,0:T(8,128)S(1)} %get-tuple-element.52) | copy-start | bytes 49156
  206.4 8.4 %collective-permute-start.4 = (bf16[1,4,2,8,128]{4,3,1,2,0:T(8,128)(2,1)S(1)}, bf16[1,4,2,8,128]{4,3,1,2,0:T(8,128)(2,1)S(1)}, u32[]{:S(2)}, u32[]{:S(2)}) collective-permute-start(bf16[1,4,2,8,128]{4,3,1,2,0:T(8,128)(2,1)S(1)} %fusion.20), channel_id=1, source_target_pairs={{0,2},{2,4},{4,6},{6,8},{8,10},{10,12},{12,14},{14,0},{1,3},{3,5},... | collective-permute-start | bytes 49160 | tf_op jit(solution)/shard_map/ppermute | solution.py:18
  206.4 8.4 %collective-permute-start.5 = (bf16[1,4,2,8,128]{4,3,1,2,0:T(8,128)(2,1)S(1)}, bf16[1,4,2,8,128]{4,3,1,2,0:T(8,128)(2,1)S(1)}, u32[]{:S(2)}, u32[]{:S(2)}) collective-permute-start(bf16[1,4,2,8,128]{4,3,1,2,0:T(8,128)(2,1)S(1)} %fusion.20), channel_id=1, source_target_pairs={{2,0},{4,2},{6,4},{8,6},{10,8},{12,10},{14,12},{0,14},{3,1},{5,3},... | collective-permute-start | bytes 49160 | tf_op jit(solution)/shard_map/ppermute | solution.py:19
  211.8 1.0 copy-start.8
  213.7 1.3 copy-start.23
  214.8 4.0 %copy-start.22 = (pred[4,9]{1,0:T(4,128)(4,1)S(1)}, pred[4,9]{1,0:T(4,128)(4,1)}, u32[]{:S(2)}) copy-start(pred[4,9]{1,0:T(4,128)(4,1)} %and_bitcast_fusion) | copy-start | bytes 112
  214.8 1.2 collective-permute-start.7
  215.5 1.3 collective-permute-start.6
  218.7 51.0 %copy-start.17 = (f32[8,1,1024]{2,0,1:T(8,128)S(1)}, f32[8,1,1024]{2,0,1:T(8,128)}, u32[]{:S(2)}) copy-start(f32[8,1,1024]{2,0,1:T(8,128)} %copy-done.16) | copy-start | bytes 98308
  291.3 3.8 %copy-start.11 = (bf16[512,128]{0,1:T(8,128)(2,1)S(1)}, bf16[512,128]{0,1:T(8,128)(2,1)}, u32[]{:S(2)}) copy-start(bf16[512,128]{0,1:T(8,128)(2,1)} %copy-done.9) | copy-start | bytes 393220
  297.0 1.0 copy-start.4
  297.0 1.0 copy-start.6
  298.0 1.4 copy-start.13
  298.0 1.4 copy-start.15
Sparse Core Ops, SparseCore 0:
  58.1 54.6 reduce-scatter.2
  214.9 54.7 reduce-scatter.4
where the time goes:
time: 308 us; the launch traced here: 307 us
  blocking collectives  136 us (44%)
  waiting for transfers between devices  87.3 us (28%)
  other arithmetic  30 us (10%)
  local copies, waits for them, and re-layouts  22.2 us (7%)
  between operations  14.9 us (5%)
  starting transfers between devices  10.7 us (3%)
  matrix products  6.26 us (2%)
    reduce_scatter x2, waiting for transfers between devices, far_field(): lax.psum_scatter(partial_coeffs, ('tile', 'wave'), scatter_dimension=0, t...  86.5 us
    all_gather x2, blocking collectives, far_field(): scaled = lax.all_gather(owner_scaled, ('tile', 'wave'), axis=0, tiled=True)  41.5 us
    psum x1, blocking collectives, per_device(): squares = lax.psum(local_sq, ('tile', 'wave'))  34.9 us
    psum x1, blocking collectives, per_device(): lax.psum((panel_sum(basis_real * image_real + basis_imag * image_imag), p...  29.8 us
    psum x1, blocking collectives, per_device(): lax.psum(panel_sum(update_real * update_real + update_imag * update_imag)...  29.5 us
    ppermute x4, starting transfers between devices, padded_2(): after = lax.ppermute(initial, axis, down)  10.1 us
  transfers between devices with their start and end apart: 10, of which 3 were waited for; matrix products, arithmetic and copies ran while one was open for 10% of the time, Pallas kernels for 0%

commit v1 on v0

--- a/solution.py
+++ b/solution.py
@@ -155,11 +155,14 @@
     image_real = image_one[:, :, 0]
     image_imag = image_one[:, :, 1]
     inner_real, inner_imag = lax.psum(
-        (
-            panel_sum(basis_real * image_real + basis_imag * image_imag),
-            panel_sum(basis_real * image_imag - basis_imag * image_real),
+        lax.psum(
+            (
+                panel_sum(basis_real * image_real + basis_imag * image_imag),
+                panel_sum(basis_real * image_imag - basis_imag * image_real),
+            ),
+            "wave",
         ),
-        ("tile", "wave"),
+        "tile",
     )
     coef_real = inner_real / panels
     coef_imag = inner_imag / panels

time: 308 us -> 298 us (0.968)
  blocking collectives: 136 us -> 126 us
    psum x1, blocking collectives: 29.8 us -> 2.48 us  [per_device(): lax.psum((panel_sum(basis_real * image_real + basis_imag * image_imag), p...]
    psum x0 -> x1, blocking collectives: none -> 17.1 us  [per_device(): lax.psum(lax.psum((panel_sum(basis_real * image_real + basis_imag * image...]
  transfers between devices with their start and end apart: 10 -> 10, of which waited for: 3 -> 3; matrix products, arithmetic and copies ran while one was open for 10% -> 11% of each run, Pallas kernels for 0% -> 0%
where the time goes in v1:
time: 298 us; the launch traced here: 297 us
  blocking collectives  126 us (42%)
  waiting for transfers between devices  87.2 us (29%)
  other arithmetic  30 us (10%)
  local copies, waits for them, and re-layouts  22.2 us (7%)
  between operations  14.9 us (5%)
  starting transfers between devices  10.7 us (4%)
  matrix products  6.26 us (2%)
    reduce_scatter x2, waiting for transfers between devices, far_field(): lax.psum_scatter(partial_coeffs, ('tile', 'wave'), scatter_dimension=0, t...  86.4 us
    all_gather x2, blocking collectives, far_field(): scaled = lax.all_gather(owner_scaled, ('tile', 'wave'), axis=0, tiled=True)  41.7 us
    psum x1, blocking collectives, per_device(): squares = lax.psum(local_sq, ('tile', 'wave'))  34.9 us
    psum x1, blocking collectives, per_device(): lax.psum(panel_sum(update_real * update_real + update_imag * update_imag)...  29.5 us
    psum x1, blocking collectives, per_device(): lax.psum(lax.psum((panel_sum(basis_real * image_real + basis_imag * image...  17.1 us
    ppermute x4, starting transfers between devices, padded_2(): after = lax.ppermute(initial, axis, down)  10.1 us
  transfers between devices with their start and end apart: 10, of which 3 were waited for; matrix products, arithmetic and copies ran while one was open for 11% of the time, Pallas kernels for 0%

profile of v1, /device:TPU:0, one launch (start us, length us, event | category | flops | bytes accessed | tf_op | source)
XLA Modules:
  0.0 296.8 jit_solution(14847924336527909222)
XLA Ops:
  7.2 1.0 add_reduce_fusion.2
  8.2 34.9 %psum.42 = f32[8]{0:T(128)S(1)} all-reduce(f32[8]{0:T(128)S(1)} %add_reduce_fusion.2), channel_id=1, replica_groups=mesh['grp'=2,'tile'=8,'wave'=2] {'tile','wave'}, use_global_device_ids=true, to_apply=%region_1.2 | all-reduce | flops 8 | bytes 64 | tf_op jit(solution)/shard_map/psum | solution.py:149
  43.7 1.4 fusion.22
  45.1 4.7 %collective-permute-start.1 = (bf16[1,4,2,8,128]{4,3,1,2,0:T(8,128)(2,1)}, bf16[1,4,2,8,128]{4,3,1,2,0:T(8,128)(2,1)}, u32[]{:S(2)}, u32[]{:S(2)}) collective-permute-start(bf16[1,4,2,8,128]{4,3,1,2,0:T(8,128)(2,1)} %fusion.22), channel_id=1, source_target_pairs={{2,0},{4,2},{6,4},{8,6},{10,8},{12,10},{14,12},{0,14},{3,1},{5,3},... | collective-permute-start | bytes 49160 | tf_op jit(solution)/shard_map/ppermute | solution.py:19
  49.9 0.8 fusion.72
  50.7 0.7 add_convert_fusion.2
  51.4 0.7 add_convert_fusion.4
  52.0 0.8 fusion.63
  52.9 1.0 fusion.16
  54.7 1.1 cosine_convert_fusion.1
  55.9 0.8 fusion.64
  56.9 1.1 pad_maximum_fusion.2
  58.7 1.6 gather_fusion
  60.3 0.9 multiply_bitcast_fusion
  61.7 1.2 copy.121
  63.0 1.3 pad_maximum_fusion.31
  64.3 1.0 constant_dynamic-slice_fusion
  65.3 0.8 copy.126
  66.2 0.8 copy.128
  67.0 0.7 copy.112
  67.8 1.2 copy.122
  69.0 0.8 reshape.723
  69.8 0.7 copy.109
  71.1 0.7 copy.115
  71.8 0.8 pad_maximum_fusion.21
  72.6 0.8 pad_maximum_fusion.18
  73.7 1.5 gather_fusion.1
  75.9 0.6 fusion.51
  76.5 36.2 %reduce-scatter.3.cloned.1.call-done = f32[8,2,1024]{2,0,1:T(8,128)} async-done(((f32[128,2,1024]{2,0,1:T(8,128)}), f32[8,2,1024]{2,0,1:T(8,128)}) %reduce-scatter.3.cloned.1.call-update) | async-done | bytes 65552 | tf_op jit(solution)/shard_map/reduce_scatter | solution.py:132
  112.8 0.8 multiply_convert_fusion.1
  113.6 20.8 %all_gather.6 = bf16[128,2,1024]{2,0,1:T(8,128)(2,1)S(1)} all-gather(bf16[8,2,1024]{2,0,1:T(8,128)(2,1)S(1)} %multiply_convert_fusion.1), channel_id=1, replica_groups=mesh['grp'=2,'tile'=8,'wave'=2] {'tile','wave'}, dimensions={0}, use_global_device_ids=true | all-gather | bytes 557056 | tf_op jit(solution)/shard_map/all_gather | solution.py:138
  134.4 0.8 slice_negate_fusion.1
  135.2 1.0 copy.123
  136.3 1.1 pad_maximum_fusion.4
  137.3 1.0 copy.124
  138.4 2.0 convolution_bitcast_fusion.1
  140.4 0.9 copy.178
  141.4 1.2 subtract_reduce_fusion.1
  142.6 0.7 copy.131
  143.4 0.9 fusion.19
  144.3 0.9 fusion.33
  145.1 2.5 all-reduce.1
  147.6 17.1 %all-reduce = (f32[8]{0:T(128)S(1)}, f32[8]{0:T(128)S(1)}) all-reduce(f32[8]{0:T(128)S(1)} %get-tuple-element.19, f32[8]{0:T(128)S(1)} %get-tuple-element.20), channel_id=1, replica_groups=mesh['grp'=2,'tile'=8,'wave'=2] {'tile'}, use_global_device_ids=true, to_apply=%region_10.12 | all-reduce | flops 16 | bytes 128 | tf_op jit(solution)/shard_map/psum | solution.py:157
  164.8 0.9 fusion.40
  165.7 0.8 fusion.45
  166.5 29.5 %psum.47 = f32[8]{0:T(128)S(1)} all-reduce(f32[8]{0:T(128)S(1)} %fusion.40), channel_id=1, replica_groups=mesh['grp'=2,'tile'=8,'wave'=2] {'tile','wave'}, use_global_device_ids=true, to_apply=%region_12.14 | all-reduce | flops 8 | bytes 64 | tf_op jit(solution)/shard_map/psum | solution.py:173
  196.1 4.7 %collective-permute-start.5 = (bf16[1,4,2,8,128]{4,3,1,2,0:T(8,128)(2,1)S(1)}, bf16[1,4,2,8,128]{4,3,1,2,0:T(8,128)(2,1)S(1)}, u32[]{:S(2)}, u32[]{:S(2)}) collective-permute-start(bf16[1,4,2,8,128]{4,3,1,2,0:T(8,128)(2,1)S(1)} %fusion.20), channel_id=1, source_target_pairs={{2,0},{4,2},{6,4},{8,6},{10,8},{12,10},{14,12},{0,14},{3,1},{5,3},... | collective-permute-start | bytes 49160 | tf_op jit(solution)/shard_map/ppermute | solution.py:19
  201.7 0.7 copy-done.8
  202.5 0.7 fusion.65
  203.4 1.1 pad_maximum_fusion.3
  204.7 0.6 pad_maximum_fusion.34
  205.9 0.7 collective-permute-done.6
  206.9 1.5 gather_fusion.2
  209.2 50.1 %reduce-scatter.5.cloned.1.call-done = f32[8,2,1024]{2,0,1:T(8,128)} async-done(((f32[128,2,1024]{2,0,1:T(8,128)}), f32[8,2,1024]{2,0,1:T(8,128)}) %reduce-scatter.5.cloned.1.call-update) | async-done | bytes 65552 | tf_op jit(solution)/shard_map/reduce_scatter | solution.py:132
  259.3 0.8 multiply_convert_fusion
  260.2 20.9 %all_gather.7 = bf16[128,2,1024]{2,0,1:T(8,128)(2,1)S(1)} all-gather(bf16[8,2,1024]{2,0,1:T(8,128)(2,1)S(1)} %multiply_convert_fusion), channel_id=1, replica_groups=mesh['grp'=2,'tile'=8,'wave'=2] {'tile','wave'}, dimensions={0}, use_global_device_ids=true | all-gather | bytes 557056 | tf_op jit(solution)/shard_map/all_gather | solution.py:138
  281.0 0.7 slice_negate_fusion
  281.8 1.0 copy.147
  282.8 1.0 pad_maximum_fusion.5
  283.8 1.0 copy.148
  284.8 2.0 convolution_bitcast_fusion
  286.8 0.9 copy.179
  287.8 1.2 subtract_reduce_fusion
  289.3 0.6 copy.155
  (158 shorter events, 7.8 us)
Async XLA Ops:
  7.2 68.3 %copy-start = (bf16[1,4,9,2,128,128]{5,4,3,2,1,0:T(8,128)(2,1)S(1)}, bf16[1,4,9,2,128,128]{5,4,3,2,1,0:T(8,128)(2,1)}, u32[]{:S(2)}) copy-start(bf16[1,4,9,2,128,128]{5,4,3,2,1,0:T(8,128)(2,1)} %param.11) | copy-start | bytes 7077892
  7.2 105.6 %reduce-scatter.3.cloned.1.call-start = ((), (), s32[]{:S(2)}) async-start(), calls=%async_computation.2 | async-start | bytes 1114112 | tf_op jit(solution)/shard_map/reduce_scatter | solution.py:132
  43.7 7.0 %copy-start.19 = (f32[8]{0:T(128)}, f32[8]{0:T(128)S(1)}, u32[]{:S(2)}) copy-start(f32[8]{0:T(128)S(1)} %get-tuple-element.70) | copy-start | bytes 100
  45.1 17.9 %collective-permute-start = (bf16[1,4,2,8,128]{4,3,1,2,0:T(8,128)(2,1)}, bf16[1,4,2,8,128]{4,3,1,2,0:T(8,128)(2,1)}, u32[]{:S(2)}, u32[]{:S(2)}) collective-permute-start(bf16[1,4,2,8,128]{4,3,1,2,0:T(8,128)(2,1)} %fusion.22), channel_id=1, source_target_pairs={{0,2},{2,4},{4,6},{6,8},{8,10},{10,12},{12,14},{14,0},{1,3},{3,5},... | collective-permute-start | bytes 49160 | tf_op jit(solution)/shard_map/ppermute | solution.py:18
  45.1 17.9 %collective-permute-start.1 = (bf16[1,4,2,8,128]{4,3,1,2,0:T(8,128)(2,1)}, bf16[1,4,2,8,128]{4,3,1,2,0:T(8,128)(2,1)}, u32[]{:S(2)}, u32[]{:S(2)}) collective-permute-start(bf16[1,4,2,8,128]{4,3,1,2,0:T(8,128)(2,1)} %fusion.22), channel_id=1, source_target_pairs={{2,0},{4,2},{6,4},{8,6},{10,8},{12,10},{14,12},{0,14},{3,1},{5,3},... | collective-permute-start | bytes 49160 | tf_op jit(solution)/shard_map/ppermute | solution.py:19
  53.9 12.3 %copy-start.1 = (f32[512,128]{0,1:T(8,128)}, f32[512,128]{0,1:T(8,128)S(1)}, u32[]{:S(2)}) copy-start(f32[512,128]{0,1:T(8,128)S(1)} %get-tuple-element.66) | copy-start | bytes 786436
  55.8 0.8 copy-start.9
  55.9 0.8 copy-start.7
  56.8 1.2 copy-start.24
  56.8 1.2 copy-start.18
  58.0 201.3 %reduce-scatter.5.cloned.1.call-start = ((), (), s32[]{:S(2)}) async-start(), calls=%async_computation.3 | async-start | bytes 1114112 | tf_op jit(solution)/shard_map/reduce_scatter | solution.py:132
  64.3 7.5 %collective-permute-start.2 = (bf16[3,1,2,8,128]{4,3,1,2,0:T(8,128)(2,1)}, bf16[3,1,2,8,128]{4,3,1,2,0:T(8,128)(2,1)}, u32[]{:S(2)}, u32[]{:S(2)}) collective-permute-start(bf16[3,1,2,8,128]{4,3,1,2,0:T(8,128)(2,1)} %get-tuple-element.58), channel_id=1, source_target_pairs={{0,1},{1,0},{2,3},{3,2},{4,5},{5,4},{6,7},{7,6},{8,9},{9,8},{10,11... | collective-permute-start | bytes 36872 | tf_op jit(solution)/shard_map/ppermute | solution.py:18
  67.7 7.5 %copy-start.21 = (pred[4,9]{1,0:T(4,128)(4,1)S(1)}, pred[4,9]{1,0:T(4,128)(4,1)}, u32[]{:S(2)}) copy-start(pred[4,9]{1,0:T(4,128)(4,1)} %and_bitcast_fusion) | copy-start | bytes 112
  69.0 43.8 %copy-start.16 = (f32[8,1,1024]{2,0,1:T(8,128)}, f32[8,1,1024]{2,0,1:T(8,128)S(1)}, u32[]{:S(2)}) copy-start(f32[8,1,1024]{2,0,1:T(8,128)S(1)} %copy.122) | copy-start | bytes 98308
  70.5 2.1 collective-permute-start.3
  134.4 4.0 %copy-start.10 = (bf16[512,128]{0,1:T(8,128)(2,1)S(1)}, bf16[512,128]{0,1:T(8,128)(2,1)}, u32[]{:S(2)}) copy-start(bf16[512,128]{0,1:T(8,128)(2,1)} %copy-done.9) | copy-start | bytes 393220
  140.3 1.0 copy-start.3
  140.3 1.0 copy-start.5
  141.4 2.0 copy-start.20
  141.4 59.6 %copy-start.2 = (f32[512,128]{0,1:T(8,128)S(1)}, f32[512,128]{0,1:T(8,128)}, u32[]{:S(2)}) copy-start(f32[512,128]{0,1:T(8,128)} %copy-done.1) | copy-start | bytes 786436
  166.4 38.1 %copy-start.12 = (f32[1,4,1,8,128]{4,3,1,2,0:T(8,128)}, f32[1,4,1,8,128]{4,3,1,2,0:T(8,128)S(1)}, u32[]{:S(2)}) copy-start(f32[1,4,1,8,128]{4,3,1,2,0:T(8,128)S(1)} %get-tuple-element.53) | copy-start | bytes 49156
  166.5 38.1 %copy-start.14 = (f32[1,4,1,8,128]{4,3,1,2,0:T(8,128)}, f32[1,4,1,8,128]{4,3,1,2,0:T(8,128)S(1)}, u32[]{:S(2)}) copy-start(f32[1,4,1,8,128]{4,3,1,2,0:T(8,128)S(1)} %get-tuple-element.54) | copy-start | bytes 49156
  196.1 8.4 %collective-permute-start.4 = (bf16[1,4,2,8,128]{4,3,1,2,0:T(8,128)(2,1)S(1)}, bf16[1,4,2,8,128]{4,3,1,2,0:T(8,128)(2,1)S(1)}, u32[]{:S(2)}, u32[]{:S(2)}) collective-permute-start(bf16[1,4,2,8,128]{4,3,1,2,0:T(8,128)(2,1)S(1)} %fusion.20), channel_id=1, source_target_pairs={{0,2},{2,4},{4,6},{6,8},{8,10},{10,12},{12,14},{14,0},{1,3},{3,5},... | collective-permute-start | bytes 49160 | tf_op jit(solution)/shard_map/ppermute | solution.py:18
  196.1 8.4 %collective-permute-start.5 = (bf16[1,4,2,8,128]{4,3,1,2,0:T(8,128)(2,1)S(1)}, bf16[1,4,2,8,128]{4,3,1,2,0:T(8,128)(2,1)S(1)}, u32[]{:S(2)}, u32[]{:S(2)}) collective-permute-start(bf16[1,4,2,8,128]{4,3,1,2,0:T(8,128)(2,1)S(1)} %fusion.20), channel_id=1, source_target_pairs={{2,0},{4,2},{6,4},{8,6},{10,8},{12,10},{14,12},{0,14},{3,1},{5,3},... | collective-permute-start | bytes 49160 | tf_op jit(solution)/shard_map/ppermute | solution.py:19
  201.5 1.0 copy-start.8
  203.4 1.3 copy-start.23
  204.5 4.0 %copy-start.22 = (pred[4,9]{1,0:T(4,128)(4,1)S(1)}, pred[4,9]{1,0:T(4,128)(4,1)}, u32[]{:S(2)}) copy-start(pred[4,9]{1,0:T(4,128)(4,1)} %and_bitcast_fusion) | copy-start | bytes 112
  204.6 1.2 collective-permute-start.7
  205.3 1.3 collective-permute-start.6
  208.4 50.9 %copy-start.17 = (f32[8,1,1024]{2,0,1:T(8,128)S(1)}, f32[8,1,1024]{2,0,1:T(8,128)}, u32[]{:S(2)}) copy-start(f32[8,1,1024]{2,0,1:T(8,128)} %copy-done.16) | copy-start | bytes 98308
  281.0 3.8 %copy-start.11 = (bf16[512,128]{0,1:T(8,128)(2,1)S(1)}, bf16[512,128]{0,1:T(8,128)(2,1)}, u32[]{:S(2)}) copy-start(bf16[512,128]{0,1:T(8,128)(2,1)} %copy-done.9) | copy-start | bytes 393220
  286.8 1.0 copy-start.4
  286.8 1.0 copy-start.6
  287.8 1.4 copy-start.13
  287.8 1.4 copy-start.15
Sparse Core Ops, SparseCore 0:
  58.1 54.6 reduce-scatter.2
  204.6 54.6 reduce-scatter.4
